TPU v7x, 32 devices: a whole 2x2x4 slice. The times are simulated.
32 devices in a mesh: tile: 8 (over y, x, core), depth: 4 (over z).
Axes of the slice: x: 2, y: 2, z: 4, core: 2. Of those that a mesh axis runs over, the one named last changes fastest.
Arguments:
- patches: float32 [512, 256, 256], P('tile', 'depth'), may hold values from -6 to 6
- patch_owner: int32 [512, 1], P('tile'), may hold values from 0 to 7; in each aligned block of 64 rows (0 to 63, 64 to 127, ...) at most 8 rows name the same one
- patch_level: int32 [512], P('tile'), may hold values from 0 to 63
- phases: float32 [512, 256, 256], P('tile', None, 'depth'), may hold values from -3.140625 to 3.140625
Outputs:
- intensity: float32 [512, 256, 256], P('tile', 'depth')
Inputs may be any that keep to these rules, and one draw needn't show every extreme that they name: `patch_owner`: among the 64 patches of one index of tile, at most 8 have the same owner.
All inputs are finite; a program needn't handle non-finite values.
Results may differ from a plain program's by a relative error of at most 0.00017.
Values sent between devices are 32-bit elements; how exact they have to be, the bound alone decides.
No kernel may reach another device: no remote copies, remote signals or barrier semaphores. Data moves between devices by JAX's collectives and lax.ppermute only.
A program may use at most 128 MiB of HBM per device.

v0:
```python
import math
import jax
import jax.numpy as jnp
from jax import lax
from jax.sharding import PartitionSpec as P

CAP = 8
HIGHEST_PRECISION = lax.Precision.HIGHEST


def tables(extent):
    indices = jnp.arange(extent, dtype=jnp.int32)
    product = indices[:, None] * indices[None, :] % extent
    angles = product.astype(jnp.float32) * (2.0 * math.pi / extent)
    return (jnp.cos(angles), jnp.sin(angles))


def right_apply(values, matrix):
    return jnp.einsum(
        "src,ck->srk",
        values,
        matrix,
        precision=HIGHEST_PRECISION,
        preferred_element_type=jnp.float32,
    )


def apply_rows(matrix, values):
    return jnp.einsum(
        "jk,skc->sjc",
        matrix,
        values,
        precision=HIGHEST_PRECISION,
        preferred_element_type=jnp.float32,
    )


def refocus_local(field, phase):
    extent = field.shape[2]
    cosine_table, sine_table = tables(extent)
    real_gain = jnp.cos(phase)
    imag_gain = jnp.sin(phase)
    col_real = right_apply(field, cosine_table)
    col_imag = -right_apply(field, sine_table)
    spec_real = apply_rows(cosine_table, col_real) + apply_rows(sine_table, col_imag)
    spec_imag = apply_rows(cosine_table, col_imag) - apply_rows(sine_table, col_real)
    prop_real = spec_real * real_gain - spec_imag * imag_gain
    prop_imag = spec_real * imag_gain + spec_imag * real_gain
    back_real = apply_rows(cosine_table, prop_real) - apply_rows(sine_table, prop_imag)
    back_imag = apply_rows(cosine_table, prop_imag) + apply_rows(sine_table, prop_real)
    field_real = right_apply(back_real, cosine_table) - right_apply(back_imag, sine_table)
    field_imag = right_apply(back_real, sine_table) + right_apply(back_imag, cosine_table)
    return (field_real * field_real + field_imag * field_imag) * (1.0 / float(extent) ** 4)


def on_device(patches, patch_owner, patch_level, phases):
    patch_count, row_count, extent = patches.shape
    levels = phases.shape[0]
    owners = lax.axis_size("tile")
    owner_column = patch_owner[:, 0]
    level_hot = (patch_level[:, None] == jnp.arange(levels, dtype=jnp.int32)[None, :]).astype(
        jnp.float32
    )
    owner_hot = (owner_column[:, None] == jnp.arange(owners, dtype=jnp.int32)[None, :]).astype(
        jnp.float32
    )
    before = jnp.tril(jnp.ones((patch_count, patch_count), jnp.float32), -1)
    rank_value = jnp.sum(
        jnp.dot(before, owner_hot, precision=HIGHEST_PRECISION, preferred_element_type=jnp.float32)
        * owner_hot,
        axis=1,
    )
    slot_index = owner_column * CAP + rank_value.astype(jnp.int32)
    slot_count = owners * CAP
    slot_hot = (jnp.arange(slot_count, dtype=jnp.int32)[:, None] == slot_index[None, :]).astype(
        jnp.float32
    )
    outgoing = jnp.dot(
        slot_hot,
        patches.reshape(patch_count, -1),
        precision=HIGHEST_PRECISION,
        preferred_element_type=jnp.float32,
    )
    outgoing = outgoing.reshape(slot_count, row_count, extent)
    chosen = jnp.dot(
        slot_hot, level_hot, precision=HIGHEST_PRECISION, preferred_element_type=jnp.float32
    )
    incoming, picked = (
        lax.all_to_all(outgoing, "tile", split_axis=0, concat_axis=0, tiled=True),
        lax.all_to_all(chosen, "tile", split_axis=0, concat_axis=0, tiled=True),
    )
    flattened = phases.reshape(levels, -1)
    phase_rows = jnp.dot(
        picked, flattened, precision=HIGHEST_PRECISION, preferred_element_type=jnp.float32
    )
    phase_rows = phase_rows.reshape(slot_count, phases.shape[1], phases.shape[2])
    phase_turned = jnp.transpose(phase_rows, (0, 2, 1))
    whole_field, whole_phase = (
        lax.all_to_all(incoming, "depth", split_axis=0, concat_axis=1, tiled=True),
        lax.all_to_all(phase_turned, "depth", split_axis=0, concat_axis=1, tiled=True),
    )
    local_result = refocus_local(whole_field, jnp.transpose(whole_phase, (0, 2, 1)))
    result = lax.all_to_all(local_result, "depth", split_axis=1, concat_axis=0, tiled=True)
    returned = lax.all_to_all(result, "tile", split_axis=0, concat_axis=0, tiled=True)
    placed = jnp.dot(
        slot_hot.T,
        returned.reshape(slot_count, -1),
        precision=HIGHEST_PRECISION,
        preferred_element_type=jnp.float32,
    )
    return placed.reshape(patch_count, row_count, extent)


def solution(mesh):
    return jax.shard_map(
        on_device,
        mesh=mesh,
        in_specs=(P("tile", "depth", None), P("tile", None), P("tile"), P("tile", None, "depth")),
        out_specs=P("tile", "depth", None),
        check_vma=False,
    )
```

profile of v0, /device:TPU:0, one launch (start us, length us, event | category | flops | bytes accessed | tf_op | source)
XLA Modules:
  0.0 528.9 jit_solution(16689904573134012535)
XLA Ops:
  0.0 0.9 fusion.42
  1.0 0.7 convert_add_fusion
  1.6 0.9 convolution_bitcast_fusion.1
  2.6 0.7 reshape.39
  3.2 5.2 all-to-all-start.2
  8.4 6.9 %fusion.3 = f32[64,64,256]{2,0,1:T(8,128)S(1)} fusion(s32[64]{0:T(128)S(1)} %convert_add_fusion, f32[8,8,64,256]{3,2,1,0:T(8,128)} %bitcast.140), kind=kOutput, calls=%fused_computation.3 | convolution fusion | flops 805310464 | bytes 8388864 | tf_op jit(solution)/shard_map/dot_general | solution.py:78
  15.3 4.4 copy.58
  19.7 0.0 all-to-all-done.2
  19.7 4.8 all-to-all-start
  24.5 6.9 %copy.62 = f32[64,256,64]{2,1,0:T(8,128)} copy(f32[64,256,64]{1,2,0:T(8,128)} %param.7) | data formatting | bytes 8388608 | tf_op args[3]
  31.4 6.9 %reshape.32 = f32[64,16384]{1,0:T(8,128)} reshape(f32[64,256,64]{2,1,0:T(8,128)} %copy.62) | data formatting | bytes 8388608 | tf_op jit(solution)/shard_map/reshape | solution.py:92
  38.3 7.4 %dot_general.79 = f32[256,64,64]{1,0,2:T(8,128)} reshape(f32[16384,64]{0,1:T(8,128)} %bitcast.134) | data formatting | bytes 8388608 | tf_op jit(solution)/shard_map/dot_general | solution.py:93
  45.6 7.3 %copy.63 = f32[256,64,64]{0,2,1:T(8,128)} copy(f32[256,64,64]{1,0,2:T(8,128)} %dot_general.79) | data formatting | bytes 8388608 | tf_op jit(solution)/shard_map/dot_general | solution.py:93
  52.9 0.5 broadcast.68
  53.5 0.6 reduce
  54.1 0.1 reshape.40
  54.2 5.5 %convolution_bitcast_fusion = f32[64,64,256]{2,0,1:T(8,128)S(1)} fusion(f32[256,64,64]{0,2,1:T(8,128)} %copy.63, f32[8,8,64]{2,1,0:T(8,128)S(1)} %reshape.40), kind=kOutput, calls=%fused_computation.33 | convolution fusion | flops 805306368 | bytes 8404992 | tf_op jit(solution)/shard_map/dot_general | solution.py:93
  59.7 4.4 copy.64
  64.1 9.5 %all-to-all-done = f32[64,64,256]{2,1,0:T(8,128)} async-done(((f32[64,64,256]{2,1,0:T(8,128)}), f32[64,64,256]{2,1,0:T(8,128)}, u32[]{:S(2)}, u32[]{:S(2)}) %all-to-all-start) | async-done | bytes 4194336 | tf_op jit(solution)/shard_map/all_to_all | solution.py:89
  73.6 96.2 %all_to_all.67 = f32[64,64,256]{2,1,0:T(8,128)} all-to-all(f32[64,64,256]{2,1,0:T(8,128)} %copy.64), channel_id=1, replica_groups=mesh['tile'=8,'depth'=4] {'depth'}, dimensions={0} | all-to-all | bytes 8388608 | tf_op jit(solution)/shard_map/all_to_all | solution.py:100
  169.8 4.8 all-to-all-start.1
  174.7 16.0 %fusion.154 = (f32[64,64,256]{2,1,0:T(8,128)S(1)}, f32[64,64,256]{2,1,0:T(8,128)S(1)}) fusion(f32[64,64,256]{2,1,0:T(8,128)} %all_to_all.67), kind=kLoop, calls=%fused_computation.145 | loop fusion | bytes 12582912 | tf_op jit(solution)/shard_map/sin | solution.py:42
  190.6 2.3 copy.65
  192.9 2.3 copy.68
  195.2 71.0 %all-to-all-done.1 = f32[64,64,256]{2,1,0:T(8,128)} async-done(((f32[64,64,256]{2,1,0:T(8,128)}), f32[64,64,256]{2,1,0:T(8,128)}, u32[]{:S(2)}, u32[]{:S(2)}) %all-to-all-start.1) | async-done | bytes 4194336 | tf_op jit(solution)/shard_map/all_to_all | solution.py:99
  266.2 2.5 copy.59
  268.7 5.2 fusion.62
  273.9 4.6 fusion.53
  278.4 5.0 fusion.50
  283.5 6.9 %fusion.60 = f32[16,256,256]{2,1,0:T(8,128)} fusion(f32[16,256,256]{1,2,0:T(8,128)S(1)} %fusion.62), kind=kOutput, calls=%fused_computation.61 | convolution fusion | flops 3222142976 | bytes 8388608 | tf_op jit(solution)/shard_map/jk,skc->sjc/dot_general | solution.py:29
  290.4 0.0 copy-start
  290.4 8.2 %fusion.31 = f32[16,256,256]{2,1,0:T(8,128)S(1)} fusion(f32[16,256,256]{2,1,0:T(8,128)S(1)} %fusion.50, f32[16,256,256]{2,1,0:T(8,128)S(1)} %fusion.53), kind=kOutput, calls=%fused_computation.35 | convolution fusion | flops 3224240128 | bytes 12582912 | tf_op jit(solution)/shard_map/jk,skc->sjc/dot_general | solution.py:29
  298.6 0.0 copy-done
  298.6 13.1 %fusion.18 = (f32[16,256,256]{2,1,0:T(8,128)S(1)}, f32[16,256,256]{2,1,0:T(8,128)S(1)}) fusion(f32[4,16,64,256]{3,2,0,1:T(8,128)S(1)} %copy-done, f32[16,256,256]{2,1,0:T(8,128)S(1)} %fusion.31, f32[4,16,64,256]{3,2,0,1:T(8,128)} %copy.68, f32[16,256,256]{2,1,0:T(8,128)} %fusion.60, f32[16,256,256]{2,1,0:T(8,128)S(1)} %fusion.53), kind=kOutput, calls=%fused_computation.20 | convolution fusion | flops 3230531584 | bytes 29360128 | tf_op jit(solution)/shard_map/jk,skc->sjc/dot_general | solution.py:29
  311.7 4.8 fusion.16
  316.5 4.4 fusion.14
  320.9 4.4 fusion.37
  325.3 8.4 %fusion.6 = f32[16,256,256]{2,1,0:T(8,128)S(1)} fusion(f32[16,256,256]{2,1,0:T(8,128)S(1)} %fusion.37), kind=kOutput, calls=%fused_computation.6 | convolution fusion | flops 3222142976 | bytes 8388608 | tf_op jit(solution)/shard_map/src,ck->srk/dot_general | solution.py:19
  333.7 8.2 %fusion.8 = f32[16,256,256]{2,1,0:T(8,128)S(1)} fusion(f32[16,256,256]{2,1,0:T(8,128)S(1)} %fusion.37), kind=kOutput, calls=%fused_computation.8 | convolution fusion | flops 3222142976 | bytes 8388608 | tf_op jit(solution)/shard_map/src,ck->srk/dot_general | solution.py:19
  342.0 4.8 fusion.34
  346.7 8.3 %fusion.10 = f32[16,256,256]{2,1,0:T(8,128)S(1)} fusion(f32[16,256,256]{2,1,0:T(8,128)S(1)} %fusion.34), kind=kOutput, calls=%fused_computation.10 | convolution fusion | flops 3222142976 | bytes 8388608 | tf_op jit(solution)/shard_map/src,ck->srk/dot_general | solution.py:19
  355.0 8.8 %add_multiply_fusion = f32[16,256,256]{2,1,0:T(8,128)S(1)} fusion(f32[16,256,256]{2,1,0:T(8,128)S(1)} %fusion.10, f32[16,256,256]{2,1,0:T(8,128)S(1)} %fusion.6, f32[16,256,256]{2,1,0:T(8,128)S(1)} %fusion.8, f32[16,256,256]{2,1,0:T(8,128)S(1)} %fusion.34), kind=kOutput, calls=%fused_computation.28 | convolution fusion | flops 3228434432 | bytes 20971520 | tf_op jit(solution)/shard_map/src,ck->srk/dot_general | solution.py:19
  363.8 2.7 copy.73
  366.5 95.3 %all_to_all.68 = f32[16,256,256]{2,0,1:T(8,128)S(1)} all-to-all(f32[16,256,256]{2,0,1:T(8,128)S(1)} %copy.73), channel_id=1, replica_groups=mesh['tile'=8,'depth'=4] {'depth'}, dimensions={1} | all-to-all | bytes 8388608 | tf_op jit(solution)/shard_map/all_to_all | solution.py:103
  461.8 2.4 copy.75
  464.2 55.0 %all_to_all.69 = f32[64,64,256]{2,1,0:T(8,128)S(1)} all-to-all(f32[64,64,256]{2,1,0:T(8,128)S(1)} %bitcast.139), channel_id=1, replica_groups=mesh['tile'=8,'depth'=4] {'tile'}, dimensions={0} | all-to-all | bytes 8388608 | tf_op jit(solution)/shard_map/all_to_all | solution.py:104
  519.2 4.8 fusion
  524.0 4.4 copy.77
  (1 shorter events, 0.0 us)
Async XLA Ops:
  3.2 16.5 %all-to-all-start.2 = ((f32[8,1,512]{2,1,0:T(1,128)}), f32[8,1,512]{2,1,0:T(1,128)S(1)}, u32[]{:S(2)}, u32[]{:S(2)}) async-start(f32[8,1,512]{2,1,0:T(1,128)} %reshape.39), calls=%async_computation.2 | async-start | bytes 32768 | tf_op jit(solution)/shard_map/all_to_all | solution.py:90
  19.7 53.9 %all-to-all-start = ((f32[64,64,256]{2,1,0:T(8,128)}), f32[64,64,256]{2,1,0:T(8,128)}, u32[]{:S(2)}, u32[]{:S(2)}) async-start(f32[64,64,256]{2,1,0:T(8,128)} %copy.58), calls=%async_computation | async-start | bytes 8388608 | tf_op jit(solution)/shard_map/all_to_all | solution.py:89
  169.8 96.4 %all-to-all-start.1 = ((f32[64,64,256]{2,1,0:T(8,128)}), f32[64,64,256]{2,1,0:T(8,128)}, u32[]{:S(2)}, u32[]{:S(2)}) async-start(f32[64,64,256]{2,1,0:T(8,128)} %all-to-all-done), calls=%async_computation.1 | async-start | bytes 8388608 | tf_op jit(solution)/shard_map/all_to_all | solution.py:99
  290.4 8.2 %copy-start = (f32[4,16,64,256]{3,2,0,1:T(8,128)S(1)}, f32[4,16,64,256]{3,2,0,1:T(8,128)}, u32[]{:S(2)}) copy-start(f32[4,16,64,256]{3,2,0,1:T(8,128)} %copy.65) | copy-start | bytes 12582916
where the time goes:
time: 535 us; the launch traced here: 529 us
  blocking collectives  246 us (46%)
  matrix products  114 us (21%)
  waiting for transfers between devices  80.5 us (15%)
  local copies, waits for them, and re-layouts  71.1 us (13%)
  starting transfers between devices  14.8 us (3%)
    all_to_all x1, blocking collectives, on_device(): lax.all_to_all(phase_turned, 'depth', split_axis=0, concat_axis=1, tiled=...  96.2 us
    all_to_all x1, blocking collectives, on_device(): lax.all_to_all(local_result, 'depth', split_axis=1, concat_axis=0, tiled=...  95.3 us
    all_to_all x1, waiting for transfers between devices, on_device(): lax.all_to_all(incoming, 'depth', split_axis=0, concat_axis=1, tiled=True)  71 us
    all_to_all x1, blocking collectives, on_device(): lax.all_to_all(result, 'tile', split_axis=0, concat_axis=0, tiled=True)  55 us
    dot_general x8, matrix products, apply_rows(): jnp.einsum('jk,skc->sjc', matrix, values, precision=HIGHEST_PRECISION, pr...  51.6 us
    dot_general x6, matrix products, right_apply(): jnp.einsum('src,ck->srk', values, matrix, precision=HIGHEST_PRECISION, pr...  43.4 us
    sin x2, local copies, waits for them, and re-layouts, refocus_local(): imag_gain = jnp.sin(phase)  18.2 us
    dot_general x2, local copies, waits for them, and re-layouts, on_device(): jnp.dot(picked, flattened, precision=HIGHEST_PRECISION, preferred_element...  14.7 us
  transfers between devices with their start and end apart: 3, of which 2 were waited for; matrix products, arithmetic and copies ran while one was open for 13% of the time, Pallas kernels for 0%

commit v1 on v0

--- a/solution.py
+++ b/solution.py
@@ -6,6 +6,22 @@
 
 CAP = 8
 HIGHEST_PRECISION = lax.Precision.HIGHEST
+
+
+def exchange_in_pairs(value, axis, split, join):
+    ways, here = (lax.axis_size(axis), lax.axis_index(axis))
+    width = value.shape[split] // ways
+    dims = list(value.shape)
+    dims[split] = width
+    height = dims[join]
+    dims[join] = height * ways
+    full = jnp.zeros(dims, value.dtype)
+    for mask in range(ways):
+        part = lax.dynamic_slice_in_dim(value, (here ^ mask) * width, width, axis=split)
+        if mask:
+            part = lax.ppermute(part, axis, [(d, d ^ mask) for d in range(ways)])
+        full = lax.dynamic_update_slice_in_dim(full, part, (here ^ mask) * height, axis=join)
+    return full
 
 
 def tables(extent):
@@ -96,7 +112,7 @@
     phase_rows = phase_rows.reshape(slot_count, phases.shape[1], phases.shape[2])
     phase_turned = jnp.transpose(phase_rows, (0, 2, 1))
     whole_field, whole_phase = (
-        lax.all_to_all(incoming, "depth", split_axis=0, concat_axis=1, tiled=True),
+        exchange_in_pairs(incoming, "depth", 0, 1),
         lax.all_to_all(phase_turned, "depth", split_axis=0, concat_axis=1, tiled=True),
     )
     local_result = refocus_local(whole_field, jnp.transpose(whole_phase, (0, 2, 1)))

time: 535 us -> 556 us (1.039)
  blocking collectives: 246 us -> 167 us
  waiting for transfers between devices: 80.5 us -> 156 us
  local copies, waits for them, and re-layouts: 71.1 us -> 84.9 us
  matrix products: 114 us -> 120 us
    ppermute x0 -> x3, waiting for transfers between devices: none -> 146 us  [exchange_in_pairs(): part = lax.ppermute(part, axis, [(d, d ^ mask) for d in range(ways)])]
    all_to_all x1 -> x0, blocking collectives: 96.2 us -> none  [on_device(): lax.all_to_all(phase_turned, 'depth', split_axis=0, concat_axis=1, tiled=...]
    all_to_all x1, waiting for transfers between devices: 71 us -> 0.01 us  [on_device(): lax.all_to_all(phase_turned, 'depth', split_axis=0, concat_axis=1, tiled=...]
    all_to_all x1, blocking collectives: 95.3 us -> 113 us  [on_device(): lax.all_to_all(local_result, 'depth', split_axis=1, concat_axis=0, tiled=...]
    dynamic_update_slice x0 -> x3, local copies, waits for them, and re-layouts: none -> 6.99 us  [exchange_in_pairs(): lax.dynamic_update_slice_in_dim(full, part, (here ^ mask) * height, axis=...]
  transfers between devices with their start and end apart: 3 -> 6, of which waited for: 2 -> 3; matrix products, arithmetic and copies ran while one was open for 13% -> 18% of each run, Pallas kernels for 0% -> 0%
where the time goes in v1:
time: 556 us; the launch traced here: 550 us
  blocking collectives  167 us (30%)
  waiting for transfers between devices  156 us (28%)
  matrix products  120 us (22%)
  local copies, waits for them, and re-layouts  84.9 us (15%)
  starting transfers between devices  19.5 us (4%)
    ppermute x3, waiting for transfers between devices, exchange_in_pairs(): part = lax.ppermute(part, axis, [(d, d ^ mask) for d in range(ways)])  146 us
    all_to_all x1, blocking collectives, on_device(): lax.all_to_all(local_result, 'depth', split_axis=1, concat_axis=0, tiled=...  113 us
    all_to_all x1, blocking collectives, on_device(): lax.all_to_all(result, 'tile', split_axis=0, concat_axis=0, tiled=True)  53.9 us
    dot_general x8, matrix products, apply_rows(): jnp.einsum('jk,skc->sjc', matrix, values, precision=HIGHEST_PRECISION, pr...  52.9 us
    dot_general x6, matrix products, right_apply(): jnp.einsum('src,ck->srk', values, matrix, precision=HIGHEST_PRECISION, pr...  48.5 us
    sin x2, local copies, waits for them, and re-layouts, refocus_local(): imag_gain = jnp.sin(phase)  18.3 us
    dot_general x2, local copies, waits for them, and re-layouts, on_device(): jnp.dot(picked, flattened, precision=HIGHEST_PRECISION, preferred_element...  14.7 us
  transfers between devices with their start and end apart: 6, of which 3 were waited for; matrix products, arithmetic and copies ran while one was open for 18% of the time, Pallas kernels for 0%

profile of v1, /device:TPU:0, one launch (start us, length us, event | category | flops | bytes accessed | tf_op | source)
XLA Modules:
  0.0 549.6 jit_solution(16091366385730930499)
XLA Ops:
  0.0 0.9 fusion.42
  1.6 0.9 convolution_bitcast_fusion.1
  3.2 5.2 all-to-all-start.1
  8.4 6.9 %fusion.3 = f32[64,64,256]{2,0,1:T(8,128)S(1)} fusion(s32[64]{0:T(128)S(1)} %convert_add_fusion, f32[8,8,64,256]{3,2,1,0:T(8,128)} %bitcast.134), kind=kOutput, calls=%fused_computation.3 | convolution fusion | flops 805310464 | bytes 8388864 | tf_op jit(solution)/shard_map/dot_general | solution.py:94
  15.3 4.4 copy.63
  19.7 4.8 all-to-all-start
  24.5 6.9 %copy.66 = f32[64,256,64]{2,1,0:T(8,128)} copy(f32[64,256,64]{1,2,0:T(8,128)} %param.7) | data formatting | bytes 8388608 | tf_op args[3]
  31.4 6.9 %reshape.32 = f32[64,16384]{1,0:T(8,128)} reshape(f32[64,256,64]{2,1,0:T(8,128)} %copy.66) | data formatting | bytes 8388608 | tf_op jit(solution)/shard_map/reshape | solution.py:108
  38.3 7.4 %dot_general.79 = f32[256,64,64]{1,0,2:T(8,128)} reshape(f32[16384,64]{0,1:T(8,128)} %bitcast.128) | data formatting | bytes 8388608 | tf_op jit(solution)/shard_map/dot_general | solution.py:109
  45.7 7.3 %copy.67 = f32[256,64,64]{0,2,1:T(8,128)} copy(f32[256,64,64]{1,0,2:T(8,128)} %dot_general.79) | data formatting | bytes 8388608 | tf_op jit(solution)/shard_map/dot_general | solution.py:109
  54.2 5.5 convolution_bitcast_fusion
  59.7 4.4 copy.68
  64.2 9.5 %all-to-all-done = f32[64,64,256]{2,1,0:T(8,128)} async-done(((f32[64,64,256]{2,1,0:T(8,128)}), f32[64,64,256]{2,1,0:T(8,128)}, u32[]{:S(2)}, u32[]{:S(2)}) %all-to-all-start) | async-done | bytes 4194336 | tf_op jit(solution)/shard_map/all_to_all | solution.py:105
  73.6 5.1 all-to-all-start.2
  78.8 2.4 broadcast_in_dim.10
  81.2 3.6 constant_dynamic-slice_fusion
  84.8 2.0 collective-permute-start
  86.8 2.3 collective-permute-start.1
  89.2 80.7 %collective-permute-done = f32[16,64,256]{2,1,0:T(8,128)} collective-permute-done((f32[16,64,256]{2,1,0:T(8,128)S(1)}, f32[16,64,256]{2,1,0:T(8,128)}, u32[]{:S(2)}, u32[]{:S(2)}) %collective-permute-start) | collective-permute-done | bytes 1048608 | tf_op jit(solution)/shard_map/ppermute | solution.py:22
  169.9 2.3 constant_dynamic-update-slice_fusion.2
  172.3 65.5 %collective-permute-done.1 = f32[16,64,256]{2,1,0:T(8,128)} collective-permute-done((f32[16,64,256]{2,1,0:T(8,128)S(1)}, f32[16,64,256]{2,1,0:T(8,128)}, u32[]{:S(2)}, u32[]{:S(2)}) %collective-permute-start.1) | collective-permute-done | bytes 1048608 | tf_op jit(solution)/shard_map/ppermute | solution.py:22
  237.8 2.4 constant_dynamic-update-slice_fusion.1
  240.2 2.3 constant_dynamic-update-slice_fusion
  242.5 7.6 %fusion.62 = f32[16,256,256]{1,2,0:T(8,128)S(1)} fusion(f32[16,256,256]{2,1,0:T(8,128)} %constant_dynamic-update-slice_fusion), kind=kOutput, calls=%fused_computation.64 | convolution fusion | flops 3222142976 | bytes 8388608 | tf_op jit(solution)/shard_map/src,ck->srk/dot_general | solution.py:35
  250.1 7.2 %fusion.53 = f32[16,256,256]{2,1,0:T(8,128)S(1)} fusion(f32[16,256,256]{2,1,0:T(8,128)} %constant_dynamic-update-slice_fusion), kind=kOutput, calls=%fused_computation.55 | convolution fusion | flops 3222142976 | bytes 8388608 | tf_op jit(solution)/shard_map/src,ck->srk/dot_general | solution.py:35
  257.3 4.4 fusion.50
  261.7 7.4 %fusion.60 = f32[16,256,256]{2,1,0:T(8,128)} fusion(f32[16,256,256]{1,2,0:T(8,128)S(1)} %fusion.62), kind=kOutput, calls=%fused_computation.62 | convolution fusion | flops 3222142976 | bytes 8388608 | tf_op jit(solution)/shard_map/jk,skc->sjc/dot_general | solution.py:45
  269.1 10.0 %fusion.31 = f32[16,256,256]{2,1,0:T(8,128)} fusion(f32[16,256,256]{2,1,0:T(8,128)S(1)} %fusion.50, f32[16,256,256]{2,1,0:T(8,128)S(1)} %fusion.53), kind=kOutput, calls=%fused_computation.35 | convolution fusion | flops 3224240128 | bytes 12582912 | tf_op jit(solution)/shard_map/jk,skc->sjc/dot_general | solution.py:45
  279.2 15.9 %fusion.154 = (f32[64,64,256]{2,1,0:T(8,128)S(1)}, f32[64,64,256]{2,1,0:T(8,128)S(1)}) fusion(f32[64,64,256]{2,1,0:T(8,128)} %all-to-all-done.2), kind=kLoop, calls=%fused_computation.152 | loop fusion | bytes 12582912 | tf_op jit(solution)/shard_map/sin | solution.py:58
  295.1 2.4 copy.69
  297.5 2.4 copy.72
  299.9 1.9 copy-done.1
  301.8 1.2 copy-done.2
  303.0 12.6 %fusion.18 = (f32[16,256,256]{2,1,0:T(8,128)S(1)}, f32[16,256,256]{2,1,0:T(8,128)S(1)}) fusion(f32[4,16,64,256]{3,2,0,1:T(8,128)} %copy.69, f32[16,256,256]{2,1,0:T(8,128)S(1)} %copy-done.2, f32[4,16,64,256]{3,2,0,1:T(8,128)} %copy.72, f32[16,256,256]{2,1,0:T(8,128)S(1)} %copy-done.3, f32[16,256,256]{2,1,0:T(8,128)S(1)} %copy-done.1), kind=kOutput, calls=%fused_computation.20 | convolution fusion | flops 3230531584 | bytes 29360128 | tf_op jit(solution)/shard_map/jk,skc->sjc/dot_general | solution.py:45
  315.6 4.8 fusion.16
  320.4 4.4 fusion.14
  324.8 4.4 fusion.37
  329.3 8.4 %fusion.6 = f32[16,256,256]{2,1,0:T(8,128)S(1)} fusion(f32[16,256,256]{2,1,0:T(8,128)S(1)} %fusion.37), kind=kOutput, calls=%fused_computation.6 | convolution fusion | flops 3222142976 | bytes 8388608 | tf_op jit(solution)/shard_map/src,ck->srk/dot_general | solution.py:35
  337.7 8.2 %fusion.8 = f32[16,256,256]{2,1,0:T(8,128)S(1)} fusion(f32[16,256,256]{2,1,0:T(8,128)S(1)} %fusion.37), kind=kOutput, calls=%fused_computation.8 | convolution fusion | flops 3222142976 | bytes 8388608 | tf_op jit(solution)/shard_map/src,ck->srk/dot_general | solution.py:35
  345.9 4.8 fusion.34
  350.7 8.3 %fusion.10 = f32[16,256,256]{2,1,0:T(8,128)S(1)} fusion(f32[16,256,256]{2,1,0:T(8,128)S(1)} %fusion.34), kind=kOutput, calls=%fused_computation.10 | convolution fusion | flops 3222142976 | bytes 8388608 | tf_op jit(solution)/shard_map/src,ck->srk/dot_general | solution.py:35
  359.0 8.8 %add_multiply_fusion = f32[16,256,256]{2,1,0:T(8,128)S(1)} fusion(f32[16,256,256]{2,1,0:T(8,128)S(1)} %fusion.10, f32[16,256,256]{2,1,0:T(8,128)S(1)} %fusion.6, f32[16,256,256]{2,1,0:T(8,128)S(1)} %fusion.8, f32[16,256,256]{2,1,0:T(8,128)S(1)} %fusion.34), kind=kOutput, calls=%fused_computation.28 | convolution fusion | flops 3228434432 | bytes 20971520 | tf_op jit(solution)/shard_map/src,ck->srk/dot_general | solution.py:35
  367.8 2.7 copy.77
  370.5 113.2 %all_to_all.49 = f32[16,256,256]{2,0,1:T(8,128)S(1)} all-to-all(f32[16,256,256]{2,0,1:T(8,128)S(1)} %copy.77), channel_id=1, replica_groups=mesh['tile'=8,'depth'=4] {'depth'}, dimensions={1} | all-to-all | bytes 8388608 | tf_op jit(solution)/shard_map/all_to_all | solution.py:119
  483.7 2.4 copy.79
  486.1 53.9 %all_to_all.50 = f32[64,64,256]{2,1,0:T(8,128)S(1)} all-to-all(f32[64,64,256]{2,1,0:T(8,128)S(1)} %bitcast.133), channel_id=1, replica_groups=mesh['tile'=8,'depth'=4] {'tile'}, dimensions={0} | all-to-all | bytes 8388608 | tf_op jit(solution)/shard_map/all_to_all | solution.py:120
  539.9 4.8 fusion
  544.7 4.4 copy.81
  (16 shorter events, 2.8 us)
Async XLA Ops:
  3.2 16.5 %all-to-all-start.1 = ((f32[8,1,512]{2,1,0:T(1,128)}), f32[8,1,512]{2,1,0:T(1,128)S(1)}, u32[]{:S(2)}, u32[]{:S(2)}) async-start(f32[8,1,512]{2,1,0:T(1,128)} %reshape.39), calls=%async_computation.1 | async-start | bytes 32768 | tf_op jit(solution)/shard_map/all_to_all | solution.py:106
  19.7 53.9 %all-to-all-start = ((f32[64,64,256]{2,1,0:T(8,128)}), f32[64,64,256]{2,1,0:T(8,128)}, u32[]{:S(2)}, u32[]{:S(2)}) async-start(f32[64,64,256]{2,1,0:T(8,128)} %copy.63), calls=%async_computation | async-start | bytes 8388608 | tf_op jit(solution)/shard_map/all_to_all | solution.py:105
  73.6 205.5 %all-to-all-start.2 = ((f32[64,64,256]{2,1,0:T(8,128)}), f32[64,64,256]{2,1,0:T(8,128)}, u32[]{:S(2)}, u32[]{:S(2)}) async-start(f32[64,64,256]{2,1,0:T(8,128)} %copy.68), calls=%async_computation.2 | async-start | bytes 8388608 | tf_op jit(solution)/shard_map/all_to_all | solution.py:116
  84.8 85.1 %collective-permute-start = (f32[16,64,256]{2,1,0:T(8,128)S(1)}, f32[16,64,256]{2,1,0:T(8,128)}, u32[]{:S(2)}, u32[]{:S(2)}) collective-permute-start(f32[16,64,256]{2,1,0:T(8,128)S(1)} %get-tuple-element.11), channel_id=1, source_target_pairs={{0,1},{1,0},{2,3},{3,2},{4,5},{5,4},{6,7},{7,6},{8,9},{9,8},{10,11... | collective-permute-start | bytes 3145736 | tf_op jit(solution)/shard_map/ppermute | solution.py:22
  86.8 151.0 %collective-permute-start.1 = (f32[16,64,256]{2,1,0:T(8,128)S(1)}, f32[16,64,256]{2,1,0:T(8,128)}, u32[]{:S(2)}, u32[]{:S(2)}) collective-permute-start(f32[16,64,256]{2,1,0:T(8,128)S(1)} %get-tuple-element.10), channel_id=1, source_target_pairs={{0,2},{1,3},{2,0},{3,1},{4,6},{5,7},{6,4},{7,5},{8,10},{9,11},{10,... | collective-permute-start | bytes 3145736 | tf_op jit(solution)/shard_map/ppermute | solution.py:22
  89.1 151.1 %collective-permute-start.2 = (f32[16,64,256]{2,1,0:T(8,128)S(1)}, f32[16,64,256]{2,1,0:T(8,128)}, u32[]{:S(2)}, u32[]{:S(2)}) collective-permute-start(f32[16,64,256]{2,1,0:T(8,128)S(1)} %get-tuple-element.9), channel_id=1, source_target_pairs={{0,3},{1,2},{2,1},{3,0},{4,7},{5,6},{6,5},{7,4},{8,11},{9,10},{10,... | collective-permute-start | bytes 3145736 | tf_op jit(solution)/shard_map/ppermute | solution.py:22
  257.3 11.8 %copy-start = (f32[16,256,256]{2,1,0:T(8,128)}, f32[16,256,256]{2,1,0:T(8,128)S(1)}, u32[]{:S(2)}) copy-start(f32[16,256,256]{2,1,0:T(8,128)S(1)} %fusion.53) | copy-start | bytes 12582916
  295.1 4.9 copy-start.3
  297.5 4.3 copy-start.1
  297.5 5.5 copy-start.2
